TPU v7x, 32 devices: a whole 2x2x4 slice. The times are simulated.
32 devices in a mesh: dom: 8 (over z, y), tm: 4 (over x, core).
Axes of the slice: x: 2, y: 2, z: 4, core: 2. Of those that a mesh axis runs over, the one named last changes fastest.
Arguments:
- panel_signal: bfloat16 [8, 8192], P('tm', 'dom'), may hold values from -6 to 6
- panel_box: int32 [8192], P('dom'), may hold values from 0 to 15
- radiation: bfloat16 [8192, 1024], P('dom'), may hold values from -0.75 to 0.75
- reception: bfloat16 [8192, 1024], P('dom'), may hold values from -0.1875 to 0.1875
- translation: bfloat16 [64, 8, 1024], P(None, None, 'dom'), may hold values from -1 to 1
- list_source: int32 [128, 8], replicated, may hold values from 0 to 127
- list_class: int32 [128, 8], replicated, may hold values from 0 to 63
- list_count: int32 [128], replicated, may hold values from 1 to 8, as said below
Outputs:
- panel_field: bfloat16 [8, 8192], P('tm', 'dom')
Inputs may be any that keep to these rules, and one draw needn't show every extreme that they name: `panel_box`: indices a panel's box among the 16 boxes of its own index of dom. Box a uses the first list_count[a] entries of its lists; the rest are padding.
All inputs are finite; a program needn't handle non-finite values.
Results may differ from a plain program's by a relative error of at most 0.0057.
Values may be sent and summed in bfloat16 or wider, within the bound.
A program may use at most 64 MiB of HBM per device.

v0:
```python
import math
import jax
import jax.numpy as jnp
from jax import lax
from jax.sharding import PartitionSpec as P

BOX_DEV = 16
J = 8


def lag_sum(kern_rows, gathered, out_steps, offset):
    entries = kern_rows.shape[0]
    lags_all = kern_rows.shape[1]
    width = kern_rows.shape[2]
    results = []
    for step_out in range(out_steps):
        total = jnp.zeros((entries, width), jnp.float32)
        for step_in in range(gathered.shape[1]):
            delay = offset + step_out - step_in
            picked = lax.dynamic_index_in_dim(
                kern_rows, jnp.clip(delay, 0, lags_all - 1), 1, keepdims=False
            )
            weight = jnp.where(delay >= 0, picked.astype(jnp.float32), 0.0)
            total = total + weight * gathered[:, step_in].astype(jnp.float32)
        results.append(total)
    return jnp.stack(results, axis=1)


def body(
    panel_signal, panel_box, radiation, reception, translation, list_source, list_class, list_count
):
    rows_own = panel_signal.shape[0]
    dirs_own = translation.shape[2]
    boxes_all = list_source.shape[0]
    classes_all = translation.shape[0]
    lags_all = translation.shape[1]
    box_onehot = (panel_box[None, :] == jnp.arange(BOX_DEV, dtype=jnp.int32)[:, None]).astype(
        jnp.bfloat16
    )
    used_rows = (jnp.arange(J, dtype=jnp.int32)[None, :] < list_count[:, None]).astype(jnp.bfloat16)
    block_size = math.gcd(boxes_all, 256)

    def translate_all(table, rays, out_steps, offset):
        width = table.shape[2]
        count_in = rays.shape[1]
        flat_table = table.reshape(classes_all, lags_all * width)
        flat_rays = rays.reshape(boxes_all, count_in * width)

        def one_block(index):
            sources = lax.dynamic_slice_in_dim(
                list_source, index * block_size, block_size, 0
            ).reshape(block_size * J)
            classes = lax.dynamic_slice_in_dim(
                list_class, index * block_size, block_size, 0
            ).reshape(block_size * J)
            keep_rows = lax.dynamic_slice_in_dim(
                used_rows, index * block_size, block_size, 0
            ).reshape(block_size * J, 1)
            kern_rows = (jnp.take(flat_table, classes, axis=0) * keep_rows).reshape(
                block_size * J, lags_all, width
            )
            gathered = jnp.take(flat_rays, sources, axis=0).reshape(block_size * J, count_in, width)
            summed = lag_sum(kern_rows, gathered, out_steps, offset)
            return jnp.sum(summed.reshape(block_size, J, out_steps, width), axis=1)

        blocks = lax.map(one_block, jnp.arange(boxes_all // block_size, dtype=jnp.int32))
        return blocks.reshape(boxes_all, out_steps, width)

    masked = panel_signal[:, None, :] * box_onehot[None]
    outgoing = jnp.einsum(
        "rbp,pk->brk", masked, radiation, preferred_element_type=jnp.float32
    ).astype(jnp.bfloat16)
    spread = lax.all_to_all(outgoing, "dom", split_axis=2, concat_axis=0, tiled=True)
    first = lax.axis_index("tm") * rows_own
    empty = jnp.zeros((boxes_all, rows_own, dirs_own), jnp.float32)
    piece = lax.all_gather(spread, "tm", axis=1, tiled=True)

    def active():
        return empty + translate_all(translation, piece, rows_own, first)

    def passive():
        return empty

    incoming = lax.cond(jnp.int32(0) <= first + rows_own - 1, active, passive)
    rays = lax.all_to_all(
        incoming.astype(jnp.bfloat16), "dom", split_axis=0, concat_axis=2, tiled=True
    )
    partial_value = jnp.einsum("brk,pk->brp", rays, reception, preferred_element_type=jnp.float32)
    field = jnp.sum(partial_value * box_onehot.astype(jnp.float32)[:, None, :], axis=0)
    return field.astype(jnp.bfloat16)


def solution(mesh):
    placed = (
        P("tm", "dom"),
        P("dom"),
        P("dom", None),
        P("dom", None),
        P(None, None, "dom"),
        P(),
        P(),
        P(),
    )
    return jax.shard_map(
        body, mesh=mesh, in_specs=placed, out_specs=P("tm", "dom"), check_vma=False
    )
```

profile of v0, /device:TPU:0, one launch (start us, length us, event | category | flops | bytes accessed | tf_op | source)
XLA Modules:
  0.0 77.4 jit_solution(18071585750592534816)
XLA Ops:
  0.0 0.8 %fusion.37 = (f32[16,1024]{1,0:T(8,128)S(1)}, bf16[16,1024]{1,0:T(8,128)(2,1)S(1)}) fusion(s32[1024]{0:T(1024)} %param.11), kind=kLoop, calls=%fused_computation.71 | loop fusion | flops 49152 | bytes 102400 | tf_op jit(solution)/shard_map/convert_element_type | solution.py:89
  0.9 0.8 copy-done
  1.6 1.2 %fusion.29 = bf16[16,2,1024]{2,0,1:T(8,128)(2,1)S(1)} fusion(bf16[1024,1024]{1,0:T(8,128)(2,1)S(1)} %copy-done, bf16[16,1024]{1,0:T(8,128)(2,1)S(1)} %get-tuple-element.91, bf16[2,1024]{1,0:T(2,128)(2,1)} %param.10), kind=kOutput, calls=%fused_computation.61 | convolution fusion | flops 67174400 | bytes 2199552 | tf_op jit(solution)/shard_map/rbp,pk->brk/dot_general | solution.py:70
  2.8 0.4 copy.42
  3.2 1.2 %reshape.173 = bf16[8,2,2048]{2,1,0:T(2,128)(2,1)} reshape(bf16[1024,2,16]{2,1,0:T(2,128)(2,1)S(1)} %bitcast.51) | data formatting | bytes 131072
  4.4 7.3 %all-to-all-start = ((bf16[8,2,2048]{2,1,0:T(2,128)(2,1)}), bf16[8,2,2048]{2,1,0:T(2,128)(2,1)S(1)}, u32[]{:S(2)}, u32[]{:S(2)}) async-start(bf16[8,2,2048]{2,1,0:T(2,128)(2,1)} %reshape.173), calls=%async_computation | async-start | bytes 131072 | tf_op jit(solution)/shard_map/all_to_all | solution.py:73
  11.8 6.8 %all-to-all-done = bf16[8,2,2048]{2,1,0:T(2,128)(2,1)S(1)} async-done(((bf16[8,2,2048]{2,1,0:T(2,128)(2,1)}), bf16[8,2,2048]{2,1,0:T(2,128)(2,1)S(1)}, u32[]{:S(2)}, u32[]{:S(2)}) %all-to-all-start) | async-done | bytes 65568 | tf_op jit(solution)/shard_map/all_to_all | solution.py:73
  18.6 0.4 reshape.174
  19.0 0.3 copy.43
  19.3 5.8 %all_gather.3 = bf16[128,8,128]{2,0,1:T(8,128)(2,1)S(1)} all-gather(bf16[128,2,128]{2,0,1:T(8,128)(2,1)S(1)} %bitcast.53), channel_id=1, replica_groups=mesh['dom'=8,'tm'=4] {'tm'}, dimensions={1}, use_global_device_ids=true | all-gather | bytes 327680 | tf_op jit(solution)/shard_map/all_gather | solution.py:76
  25.1 39.9 %conditional.1 = (bf16[128,2,128]{2,0,1:T(8,128)(2,1)S(1)}) conditional(s32[]{:T(128)} %convert_element_type.158, () %tuple.13, (s32[]{:T(128)}, s32[128,8]{0,1:T(8,128)S(1)}, bf16[64,8,128]{2,1,0:T(8,128)(2,1)S(1)}, bf16[128,8]{1,0:T(8,128)(2,1)S(1)}, s32[128,8]{0,1:T(8,128)S(1)}, /*index=5*/bf16[128,8,128]{2,0,1:T(8,128)(2,1)S(1)}) %tuple.27), branch_computations={%region_0.0_spmd, %region_1.3_spmd} | conditional | flops 13881379 | bytes 45001176 | solution.py:84
  25.6 5.3 %gather_fusion = bf16[1024,1024]{1,0:T(8,128)(2,1)} fusion(bf16[64,1024]{1,0:T(8,128)(2,1)S(1)} %bitcast.48, s32[1024]{0:T(1024)S(1)} %broadcast_clamp_fusion.1), kind=kCustom, calls=%fused_computation | custom fusion | bytes 4198400 | tf_op jit(solution)/shard_map/cond/branch_1_fun/while/body/eval_jaxpr/jit(_take)/gather | solution.py:59
  30.9 3.9 %copy.38 = bf16[1024,1024]{0,1:T(8,128)(2,1)} copy(bf16[1024,1024]{1,0:T(8,128)(2,1)} %gather_fusion) | data formatting | bytes 4194304 | tf_op jit(solution)/shard_map/cond/branch_1_fun/while/body/eval_jaxpr/jit(_take)/gather | solution.py:59
  34.8 3.9 %copy.39 = bf16[1024,8,128]{2,0,1:T(8,128)(2,1)} copy(bf16[1024,8,128]{0,2,1:T(8,128)(2,1)} %bitcast.49) | data formatting | bytes 4194304 | tf_op jit(solution)/shard_map/cond/branch_1_fun/while/body/eval_jaxpr/jit(_take)/gather | solution.py:59
  39.0 3.3 %select_multiply_fusion = bf16[1024,8,128]{2,0,1:T(8,128)(2,1)} fusion(bf16[1024,8,128]{2,0,1:T(8,128)(2,1)} %copy.39, pred[1024]{0:T(1024)(128)(4,1)S(1)} %get-tuple-element.89, bf16[1024]{0:T(1024)(128)(2,1)S(1)} %mul.98), kind=kLoop, calls=%fused_computation.2 | loop fusion | flops 2097152 | bytes 4197376 | tf_op jit(solution)/shard_map/cond/branch_1_fun/while/body/eval_jaxpr/mul | solution.py:59
  42.4 5.4 %gather_fusion.1 = bf16[1024,1024]{1,0:T(8,128)(2,1)} fusion(bf16[128,1024]{1,0:T(8,128)(2,1)S(1)} %copy_bitcast_fusion, s32[1024]{0:T(1024)S(1)} %broadcast_clamp_fusion), kind=kCustom, calls=%fused_computation.1 | custom fusion | bytes 4198400 | tf_op jit(solution)/shard_map/cond/branch_1_fun/while/body/eval_jaxpr/jit(_take)/gather | solution.py:62
  47.7 3.9 %copy.40 = bf16[1024,1024]{0,1:T(8,128)(2,1)} copy(bf16[1024,1024]{1,0:T(8,128)(2,1)} %gather_fusion.1) | data formatting | bytes 4194304 | tf_op jit(solution)/shard_map/cond/branch_1_fun/while/body/eval_jaxpr/jit(_take)/gather | solution.py:62
  51.7 3.9 %copy.41 = bf16[1024,8,128]{2,0,1:T(8,128)(2,1)} copy(bf16[1024,8,128]{0,2,1:T(8,128)(2,1)} %bitcast.50) | data formatting | bytes 4194304 | tf_op jit(solution)/shard_map/cond/branch_1_fun/while/body/eval_jaxpr/jit(_take)/gather | solution.py:62
  55.6 3.2 %broadcast_select_fusion = bf16[1024,8,128]{2,0,1:T(8,128)(2,1)} fusion(bf16[1024,8,128]{2,0,1:T(8,128)(2,1)} %copy.41, pred[1024]{0:T(1024)(128)(4,1)S(1)} %get-tuple-element.88), kind=kLoop, calls=%fused_computation.3 | loop fusion | flops 1048576 | bytes 4195328 | tf_op jit(solution)/shard_map/cond/branch_1_fun/while/body/eval_jaxpr/jit(_take)/select_n | solution.py:62
  58.7 3.0 %fusion.15 = f32[128,8,1,128]{3,1,0,2:T(8,128)S(1)} fusion(bf16[1024,8,128]{2,0,1:T(8,128)(2,1)} %select_multiply_fusion, s32[]{:T(128)S(6)} %min.50, pred[]{:T(512)S(6)} %ge.70, pred[]{:T(512)S(6)} %ge.68, pred[]{:T(512)S(6)} %ge.67, pred[]{:T(512)S(6)} %ge.66, pred[]{:T(512)S(6)} %ge.65, pred[]{:T(512)S(6)} %ge.64, pred[]{:T(512)S(6)} %ge.63, pred[]{:T(512)S(6)} %ge.60, ...), kind=kLoop, calls=%fused_computation.36 | loop fusion | flops 5111808 | bytes 4718632 | tf_op jit(solution)/shard_map/cond/branch_1_fun/while/body/eval_jaxpr/stack | solution.py:26
  61.7 3.0 %fusion.7 = f32[128,8,1,128]{3,1,0,2:T(8,128)S(1)} fusion(bf16[1024,8,128]{2,0,1:T(8,128)(2,1)} %select_multiply_fusion, s32[]{:T(128)S(6)} %min.49, pred[]{:T(512)S(6)} %ge.69, pred[]{:T(512)S(6)} %ge.68, pred[]{:T(512)S(6)} %ge.67, pred[]{:T(512)S(6)} %ge.66, pred[]{:T(512)S(6)} %ge.65, pred[]{:T(512)S(6)} %ge.64, pred[]{:T(512)S(6)} %ge.63, pred[]{:T(512)S(6)} %ge.60, ...), kind=kLoop, calls=%fused_computation.28 | loop fusion | flops 5111808 | bytes 4718632 | tf_op jit(solution)/shard_map/cond/branch_1_fun/while/body/eval_jaxpr/stack | solution.py:26
  64.8 0.3 maximum_reduce_fusion
  65.1 9.3 %all_to_all.36 = bf16[128,2,128]{2,1,0:T(2,128)(2,1)S(1)} all-to-all(bf16[128,2,128]{2,1,0:T(2,128)(2,1)S(1)} %copy.55), channel_id=1, replica_groups=mesh['dom'=8,'tm'=4] {'dom'}, dimensions={0} | all-to-all | bytes 131072 | tf_op jit(solution)/shard_map/all_to_all | solution.py:85
  74.5 2.9 %fusion.26 = bf16[2,1024]{1,0:T(2,128)(2,1)} fusion(bf16[16,2,1024]{2,0,1:T(8,128)(2,1)S(1)} %all_to_all.33, bf16[1024,1024]{1,0:T(8,128)(2,1)} %param.13, f32[16,1024]{1,0:T(8,128)S(1)} %get-tuple-element.90), kind=kOutput, calls=%fused_computation.60 | convolution fusion | flops 67172352 | bytes 2232320 | tf_op jit(solution)/shard_map/brk,pk->brp/dot_general | solution.py:88
  (26 shorter events, 1.0 us)
Async XLA Ops:
  0.0 1.6 %copy-start = (bf16[1024,1024]{1,0:T(8,128)(2,1)S(1)}, bf16[1024,1024]{1,0:T(8,128)(2,1)}, u32[]{:S(2)}) copy-start(bf16[1024,1024]{1,0:T(8,128)(2,1)} %param.12) | copy-start | bytes 6291460
  0.0 11.7 %copy-start.4 = (s32[128]{0:T(128)S(1)}, s32[128]{0:T(128)}, u32[]{:S(2)}) copy-start(s32[128]{0:T(128)} %param.17) | copy-start | bytes 1540
  1.6 23.5 %copy-start.1 = (bf16[64,8,128]{2,1,0:T(8,128)(2,1)S(1)}, bf16[64,8,128]{2,1,0:T(8,128)(2,1)}, u32[]{:S(2)}) copy-start(bf16[64,8,128]{2,1,0:T(8,128)(2,1)} %param.14) | copy-start | bytes 393220
  1.6 23.5 %copy-start.2 = (s32[128,8]{0,1:T(8,128)S(1)}, s32[128,8]{0,1:T(8,128)}, u32[]{:S(2)}) copy-start(s32[128,8]{0,1:T(8,128)} %param.16) | copy-start | bytes 12292
  1.6 23.5 %copy-start.3 = (s32[128,8]{0,1:T(8,128)S(1)}, s32[128,8]{0,1:T(8,128)}, u32[]{:S(2)}) copy-start(s32[128,8]{0,1:T(8,128)} %param.15) | copy-start | bytes 12292
  4.4 14.2 %all-to-all-start = ((bf16[8,2,2048]{2,1,0:T(2,128)(2,1)}), bf16[8,2,2048]{2,1,0:T(2,128)(2,1)S(1)}, u32[]{:S(2)}, u32[]{:S(2)}) async-start(bf16[8,2,2048]{2,1,0:T(2,128)(2,1)} %reshape.173), calls=%async_computation | async-start | bytes 131072 | tf_op jit(solution)/shard_map/all_to_all | solution.py:73
where the time goes:
time: 78 us; the launch traced here: 77.4 us
  local copies, waits for them, and re-layouts  30.3 us (39%)
  blocking collectives  15.1 us (19%)
  other arithmetic  13.7 us (18%)
  starting transfers between devices  7.31 us (9%)
  waiting for transfers between devices  6.81 us (9%)
  matrix products  4.12 us (5%)
    gather x3, local copies, waits for them, and re-layouts, one_block(): jnp.take(flat_rays, sources, axis=0)  13.2 us
    gather x3, local copies, waits for them, and re-layouts, one_block(): jnp.take(flat_table, classes, axis=0) * keep_rows  13.2 us
    all_to_all x1, blocking collectives, body(): lax.all_to_all(incoming.astype(jnp.bfloat16), 'dom', split_axis=0, concat...  9.29 us
    all_to_all x1, starting transfers between devices, body(): lax.all_to_all(outgoing, 'dom', split_axis=2, concat_axis=0, tiled=True)  7.31 us
    all_to_all x1, waiting for transfers between devices, body(): lax.all_to_all(outgoing, 'dom', split_axis=2, concat_axis=0, tiled=True)  6.81 us
    another operation x2, other arithmetic, lag_sum(): return jnp.stack(results, axis=1)  6.01 us
    all_gather x1, blocking collectives, body(): piece = lax.all_gather(spread, 'tm', axis=1, tiled=True)  5.78 us
    mul x1, other arithmetic, one_block(): jnp.take(flat_table, classes, axis=0) * keep_rows  3.27 us
  transfers between devices with their start and end apart: 1, of which 1 were waited for; matrix products, arithmetic and copies ran while one was open for 0% of the time, Pallas kernels for 0%

commit v1 on v0

--- a/solution.py
+++ b/solution.py
@@ -6,6 +6,14 @@
 
 BOX_DEV = 16
 J = 8
+
+
+def time_classes_for(obj):
+    reached = lax.axis_size("dom")
+    parts_out = jnp.stack(jnp.split(obj, reached, axis=0))
+    return jnp.concatenate(
+        lax.all_to_all(parts_out, axis_name="dom", split_axis=0, concat_axis=0), axis=2
+    )
 
 
 def lag_sum(kern_rows, gathered, out_steps, offset):
@@ -82,9 +90,7 @@
         return empty
 
     incoming = lax.cond(jnp.int32(0) <= first + rows_own - 1, active, passive)
-    rays = lax.all_to_all(
-        incoming.astype(jnp.bfloat16), "dom", split_axis=0, concat_axis=2, tiled=True
-    )
+    rays = time_classes_for(incoming.astype(jnp.bfloat16))
     partial_value = jnp.einsum("brk,pk->brp", rays, reception, preferred_element_type=jnp.float32)
     field = jnp.sum(partial_value * box_onehot.astype(jnp.float32)[:, None, :], axis=0)
     return field.astype(jnp.bfloat16)

time: 78 us -> 78 us (level)
    unnamed x12 -> x19, local copies, waits for them, and re-layouts: 2.32 us -> 2.37 us
where the time goes in v1:
time: 78 us; the launch traced here: 77.3 us
  local copies, waits for them, and re-layouts  30.2 us (39%)
  blocking collectives  15.1 us (19%)
  other arithmetic  13.7 us (18%)
  starting transfers between devices  7.31 us (9%)
  waiting for transfers between devices  6.81 us (9%)
  matrix products  4.12 us (5%)
    gather x3, local copies, waits for them, and re-layouts, one_block(): jnp.take(flat_rays, sources, axis=0)  13.2 us
    gather x3, local copies, waits for them, and re-layouts, one_block(): jnp.take(flat_table, classes, axis=0) * keep_rows  13.1 us
    all_to_all x1, blocking collectives, time_classes_for(): lax.all_to_all(parts_out, axis_name='dom', split_axis=0, concat_axis=0)  9.29 us
    all_to_all x1, starting transfers between devices, body(): lax.all_to_all(outgoing, 'dom', split_axis=2, concat_axis=0, tiled=True)  7.31 us
    all_to_all x1, waiting for transfers between devices, body(): lax.all_to_all(outgoing, 'dom', split_axis=2, concat_axis=0, tiled=True)  6.81 us
    another operation x2, other arithmetic, lag_sum(): return jnp.stack(results, axis=1)  6.05 us
    all_gather x1, blocking collectives, body(): piece = lax.all_gather(spread, 'tm', axis=1, tiled=True)  5.78 us
    mul x1, other arithmetic, one_block(): jnp.take(flat_table, classes, axis=0) * keep_rows  3.26 us
  transfers between devices with their start and end apart: 1, of which 1 were waited for; matrix products, arithmetic and copies ran while one was open for 0% of the time, Pallas kernels for 0%

profile of v1, /device:TPU:0, one launch (start us, length us, event | category | flops | bytes accessed | tf_op | source)
XLA Modules:
  0.0 77.3 jit_solution(4245781367347944511)
XLA Ops:
  0.0 0.8 %fusion.39 = (f32[16,1024]{1,0:T(8,128)S(1)}, bf16[16,1024]{1,0:T(8,128)(2,1)S(1)}) fusion(s32[1024]{0:T(1024)} %param.11), kind=kLoop, calls=%fused_computation.87 | loop fusion | flops 49152 | bytes 102400 | tf_op jit(solution)/shard_map/convert_element_type | solution.py:95
  0.9 0.8 copy-done
  1.6 1.2 %fusion.29 = bf16[16,2,1024]{2,0,1:T(8,128)(2,1)S(1)} fusion(bf16[1024,1024]{1,0:T(8,128)(2,1)S(1)} %copy-done, bf16[16,1024]{1,0:T(8,128)(2,1)S(1)} %get-tuple-element.146, bf16[2,1024]{1,0:T(2,128)(2,1)} %param.10), kind=kOutput, calls=%fused_computation.69 | convolution fusion | flops 67174400 | bytes 2199552 | tf_op jit(solution)/shard_map/rbp,pk->brk/dot_general | solution.py:78
  2.8 0.4 copy.34
  3.2 1.2 %reshape.192 = bf16[8,2,2048]{2,1,0:T(2,128)(2,1)} reshape(bf16[1024,2,16]{2,1,0:T(2,128)(2,1)S(1)} %bitcast.66) | data formatting | bytes 131072
  4.4 7.3 %all-to-all-start = ((bf16[8,2,2048]{2,1,0:T(2,128)(2,1)}), bf16[8,2,2048]{2,1,0:T(2,128)(2,1)S(1)}, u32[]{:S(2)}, u32[]{:S(2)}) async-start(bf16[8,2,2048]{2,1,0:T(2,128)(2,1)} %reshape.192), calls=%async_computation | async-start | bytes 131072 | tf_op jit(solution)/shard_map/all_to_all | solution.py:81
  11.8 6.8 %all-to-all-done = bf16[8,2,2048]{2,1,0:T(2,128)(2,1)S(1)} async-done(((bf16[8,2,2048]{2,1,0:T(2,128)(2,1)}), bf16[8,2,2048]{2,1,0:T(2,128)(2,1)S(1)}, u32[]{:S(2)}, u32[]{:S(2)}) %all-to-all-start) | async-done | bytes 65568 | tf_op jit(solution)/shard_map/all_to_all | solution.py:81
  18.6 0.4 reshape.193
  19.0 0.3 copy.35
  19.3 5.8 %all_gather.3 = bf16[128,8,128]{2,0,1:T(8,128)(2,1)S(1)} all-gather(bf16[128,2,128]{2,0,1:T(8,128)(2,1)S(1)} %bitcast.68), channel_id=1, replica_groups=mesh['dom'=8,'tm'=4] {'tm'}, dimensions={1}, use_global_device_ids=true | all-gather | bytes 327680 | tf_op jit(solution)/shard_map/all_gather | solution.py:84
  25.1 39.9 %conditional.1 = (bf16[1,16,2,128]{3,1,2,0:T(8,128)(2,1)S(1)}, bf16[1,16,2,128]{3,1,2,0:T(8,128)(2,1)S(1)}, bf16[1,16,2,128]{3,1,2,0:T(8,128)(2,1)S(1)}, bf16[1,...) conditional(s32[]{:T(128)} %convert_element_type.188, () %tuple.21, ...), branch_computations={%region_0.0_spmd, %region_1.3_spmd} | conditional | flops 13881379 | bytes 45132304 | solution.py:92
  25.5 5.3 %gather_fusion = bf16[1024,1024]{1,0:T(8,128)(2,1)} fusion(bf16[64,1024]{1,0:T(8,128)(2,1)S(1)} %bitcast.63, s32[1024]{0:T(1024)S(1)} %broadcast_clamp_fusion.1), kind=kCustom, calls=%fused_computation | custom fusion | bytes 4198400 | tf_op jit(solution)/shard_map/cond/branch_1_fun/while/body/eval_jaxpr/jit(_take)/gather | solution.py:67
  30.9 3.9 %copy.30 = bf16[1024,1024]{0,1:T(8,128)(2,1)} copy(bf16[1024,1024]{1,0:T(8,128)(2,1)} %gather_fusion) | data formatting | bytes 4194304 | tf_op jit(solution)/shard_map/cond/branch_1_fun/while/body/eval_jaxpr/jit(_take)/gather | solution.py:67
  34.8 3.9 %copy.31 = bf16[1024,8,128]{2,0,1:T(8,128)(2,1)} copy(bf16[1024,8,128]{0,2,1:T(8,128)(2,1)} %bitcast.64) | data formatting | bytes 4194304 | tf_op jit(solution)/shard_map/cond/branch_1_fun/while/body/eval_jaxpr/jit(_take)/gather | solution.py:67
  39.0 3.3 %select_multiply_fusion = bf16[1024,8,128]{2,0,1:T(8,128)(2,1)} fusion(bf16[1024,8,128]{2,0,1:T(8,128)(2,1)} %copy.31, pred[1024]{0:T(1024)(128)(4,1)S(1)} %get-tuple-element.144, bf16[1024]{0:T(1024)(128)(2,1)S(1)} %mul.115), kind=kLoop, calls=%fused_computation.2 | loop fusion | flops 2097152 | bytes 4197376 | tf_op jit(solution)/shard_map/cond/branch_1_fun/while/body/eval_jaxpr/mul | solution.py:67
  42.3 5.4 %gather_fusion.1 = bf16[1024,1024]{1,0:T(8,128)(2,1)} fusion(bf16[128,1024]{1,0:T(8,128)(2,1)S(1)} %copy_bitcast_fusion, s32[1024]{0:T(1024)S(1)} %broadcast_clamp_fusion), kind=kCustom, calls=%fused_computation.1 | custom fusion | bytes 4198400 | tf_op jit(solution)/shard_map/cond/branch_1_fun/while/body/eval_jaxpr/jit(_take)/gather | solution.py:70
  47.7 3.9 %copy.32 = bf16[1024,1024]{0,1:T(8,128)(2,1)} copy(bf16[1024,1024]{1,0:T(8,128)(2,1)} %gather_fusion.1) | data formatting | bytes 4194304 | tf_op jit(solution)/shard_map/cond/branch_1_fun/while/body/eval_jaxpr/jit(_take)/gather | solution.py:70
  51.6 3.9 %copy.33 = bf16[1024,8,128]{2,0,1:T(8,128)(2,1)} copy(bf16[1024,8,128]{0,2,1:T(8,128)(2,1)} %bitcast.65) | data formatting | bytes 4194304 | tf_op jit(solution)/shard_map/cond/branch_1_fun/while/body/eval_jaxpr/jit(_take)/gather | solution.py:70
  55.5 3.2 %broadcast_select_fusion = bf16[1024,8,128]{2,0,1:T(8,128)(2,1)} fusion(bf16[1024,8,128]{2,0,1:T(8,128)(2,1)} %copy.33, pred[1024]{0:T(1024)(128)(4,1)S(1)} %get-tuple-element.143), kind=kLoop, calls=%fused_computation.3 | loop fusion | flops 1048576 | bytes 4195328 | tf_op jit(solution)/shard_map/cond/branch_1_fun/while/body/eval_jaxpr/jit(_take)/select_n | solution.py:70
  58.7 3.0 %fusion.15 = f32[128,8,1,128]{3,1,0,2:T(8,128)S(1)} fusion(bf16[1024,8,128]{2,0,1:T(8,128)(2,1)} %select_multiply_fusion, s32[]{:T(128)S(6)} %min.66, pred[]{:T(512)S(6)} %ge.88, pred[]{:T(512)S(6)} %ge.86, pred[]{:T(512)S(6)} %ge.85, pred[]{:T(512)S(6)} %ge.84, pred[]{:T(512)S(6)} %ge.83, pred[]{:T(512)S(6)} %ge.82, pred[]{:T(512)S(6)} %ge.81, pred[]{:T(512)S(6)} %ge.78, ...), kind=kLoop, calls=%fused_computation.36 | loop fusion | flops 5111808 | bytes 4718632 | tf_op jit(solution)/shard_map/cond/branch_1_fun/while/body/eval_jaxpr/stack | solution.py:34
  61.6 3.1 %fusion.7 = f32[128,8,1,128]{3,1,0,2:T(8,128)S(1)} fusion(bf16[1024,8,128]{2,0,1:T(8,128)(2,1)} %select_multiply_fusion, s32[]{:T(128)S(6)} %min.65, pred[]{:T(512)S(6)} %ge.87, pred[]{:T(512)S(6)} %ge.86, pred[]{:T(512)S(6)} %ge.85, pred[]{:T(512)S(6)} %ge.84, pred[]{:T(512)S(6)} %ge.83, pred[]{:T(512)S(6)} %ge.82, pred[]{:T(512)S(6)} %ge.81, pred[]{:T(512)S(6)} %ge.78, ...), kind=kLoop, calls=%fused_computation.28 | loop fusion | flops 5111808 | bytes 4718632 | tf_op jit(solution)/shard_map/cond/branch_1_fun/while/body/eval_jaxpr/stack | solution.py:34
  64.7 0.3 maximum_reduce_fusion
  65.1 9.3 %all_to_all.23 = bf16[8,16,2,128]{3,1,2,0:T(8,128)(2,1)S(1)} all-to-all(bf16[8,16,2,128]{3,1,2,0:T(8,128)(2,1)S(1)} %constant_dynamic-update-slice_fusion), channel_id=1, replica_groups=mesh['dom'=8,'tm'=4] {'dom'}, dimensions={0} | all-to-all | bytes 131072 | tf_op jit(solution)/shard_map/all_to_all | solution.py:15
  74.4 2.9 %fusion.26 = bf16[2,1024]{1,0:T(2,128)(2,1)} fusion(bf16[1024,1024]{1,0:T(8,128)(2,1)} %param.13, f32[16,1024]{1,0:T(8,128)S(1)} %get-tuple-element.145, bf16[8,16,2,128]{3,1,2,0:T(8,128)(2,1)S(1)} %all_to_all.23), kind=kOutput, calls=%fused_computation.68 | convolution fusion | flops 67172352 | bytes 2232320 | tf_op jit(solution)/shard_map/brk,pk->brp/dot_general | solution.py:94
  (32 shorter events, 0.9 us)
Async XLA Ops:
  0.0 1.6 %copy-start = (bf16[1024,1024]{1,0:T(8,128)(2,1)S(1)}, bf16[1024,1024]{1,0:T(8,128)(2,1)}, u32[]{:S(2)}) copy-start(bf16[1024,1024]{1,0:T(8,128)(2,1)} %param.12) | copy-start | bytes 6291460
  0.0 11.7 %copy-start.4 = (s32[128]{0:T(128)S(1)}, s32[128]{0:T(128)}, u32[]{:S(2)}) copy-start(s32[128]{0:T(128)} %param.17) | copy-start | bytes 1540
  1.6 23.5 %copy-start.1 = (bf16[64,8,128]{2,1,0:T(8,128)(2,1)S(1)}, bf16[64,8,128]{2,1,0:T(8,128)(2,1)}, u32[]{:S(2)}) copy-start(bf16[64,8,128]{2,1,0:T(8,128)(2,1)} %param.14) | copy-start | bytes 393220
  1.6 23.5 %copy-start.2 = (s32[128,8]{0,1:T(8,128)S(1)}, s32[128,8]{0,1:T(8,128)}, u32[]{:S(2)}) copy-start(s32[128,8]{0,1:T(8,128)} %param.16) | copy-start | bytes 12292
  1.6 23.5 %copy-start.3 = (s32[128,8]{0,1:T(8,128)S(1)}, s32[128,8]{0,1:T(8,128)}, u32[]{:S(2)}) copy-start(s32[128,8]{0,1:T(8,128)} %param.15) | copy-start | bytes 12292
  4.4 14.2 %all-to-all-start = ((bf16[8,2,2048]{2,1,0:T(2,128)(2,1)}), bf16[8,2,2048]{2,1,0:T(2,128)(2,1)S(1)}, u32[]{:S(2)}, u32[]{:S(2)}) async-start(bf16[8,2,2048]{2,1,0:T(2,128)(2,1)} %reshape.192), calls=%async_computation | async-start | bytes 131072 | tf_op jit(solution)/shard_map/all_to_all | solution.py:81
